TPU v7x, 32 devices: a whole 2x2x4 slice. The times are simulated.
32 devices in a mesh: seq: 4 (over x, core), mp: 8 (over z, y).
Axes of the slice: x: 2, y: 2, z: 4, core: 2. Of those that a mesh axis runs over, the one named last changes fastest.
Arguments:
- signal: bfloat16 [2048, 8192], P('seq', 'mp'), may hold values from -6 to 6
- gate_input: bfloat16 [2048, 8192], P('seq', 'mp'), may hold values from -6 to 6
- input_map: bfloat16 [2048, 128], P('seq'), may hold values from -0.5 to 0.5
- output_map: bfloat16 [2048, 128], P('seq'), may hold values from -6 to 6
- log_decay: float32 [2048, 128], P('seq', 'mp'), may hold values from -1 to 0
- step_size: float32 [2048, 128], P('seq', 'mp'), may hold values from 0.003 to 0.03
- skip_gain: float32 [128], P('mp'), may hold values from 0.1 to 1.9
- norm_gain: float32 [8192], P('mp'), may hold values from 0.1 to 1.9
- out_weight: bfloat16 [8192, 8192], P('mp'), may hold values from -0.09375 to 0.09375
Outputs:
- mixed_out: bfloat16 [2048, 8192], P('seq', 'mp')
All inputs are finite; a program needn't handle non-finite values.
Results may differ from a plain program's by a relative error of at most 0.024.
Values may be sent and summed in bfloat16 or wider, within the bound.
A program may use at most 64 MiB of HBM per device.

v0:
```python
import jax
import jax.numpy as jnp
from jax import lax
from jax.sharding import PartitionSpec as P

BLOCK = 256
INNER = 8192


def from_behind(value, axis, steps):
    count = lax.axis_size(axis)
    leading, last = (max(0, -steps), min(count, count - steps))
    return lax.ppermute(value, axis, [(source, source + steps) for source in range(leading, last)])


def on_device(
    signal,
    gate_input,
    input_map,
    output_map,
    log_decay,
    step_size,
    skip_gain,
    norm_gain,
    out_weight,
):
    local_tokens = signal.shape[0]
    inner_width = signal.shape[1]
    heads_here = log_decay.shape[1]
    head_width = inner_width // heads_here
    state_width = input_map.shape[1]
    block_count = local_tokens // BLOCK
    signal_blk = signal.reshape(block_count, BLOCK, heads_here, head_width)
    keys_blk = input_map.reshape(block_count, BLOCK, state_width)
    query_blk = output_map.reshape(block_count, BLOCK, state_width)
    decay_blk = log_decay.reshape(block_count, BLOCK, heads_here)
    steps_blk = step_size.reshape(block_count, BLOCK, heads_here)
    cumulative = jnp.cumsum(decay_blk, axis=1)
    scores = jnp.einsum("btn,bsn->bts", query_blk, keys_blk, preferred_element_type=jnp.float32)
    cum_heads = jnp.swapaxes(cumulative, 1, 2)
    log_gaps = cum_heads[:, :, :, None] - cum_heads[:, :, None, :]
    causal = jnp.arange(BLOCK)[:, None] >= jnp.arange(BLOCK)[None, :]
    decays = jnp.exp(jnp.where(causal, log_gaps, -jnp.inf))
    weights = (scores[:, None] * decays * jnp.swapaxes(steps_blk, 1, 2)[:, :, None, :]).astype(
        jnp.bfloat16
    )
    inner_part = jnp.einsum(
        "bhts,bshp->bthp", weights, signal_blk, preferred_element_type=jnp.float32
    )
    feed_rows = (
        signal_blk * (steps_blk * jnp.exp(cumulative[:, -1:, :] - cumulative))[..., None]
    ).astype(jnp.bfloat16)
    local_state = jnp.einsum(
        "bshp,bsn->bhpn", feed_rows, keys_blk, preferred_element_type=jnp.float32
    )
    block_total = cumulative[:, -1, :]
    dev_total = jnp.sum(block_total, axis=0)
    running = jnp.zeros((heads_here, head_width, state_width), jnp.float32)
    for number in range(block_count):
        running = jnp.exp(block_total[number])[:, None, None] * running + local_state[number]
    dev_state = running

    def relay_step(number, incoming):
        outgoing = jnp.exp(dev_total)[:, None, None] * incoming + dev_state
        return from_behind(outgoing.astype(jnp.bfloat16), "seq", 1).astype(outgoing.dtype)

    incoming = lax.fori_loop(0, lax.axis_size("seq") - 1, relay_step, jnp.zeros_like(dev_state))
    running = incoming
    carried = []
    for number in range(block_count):
        carried.append(running)
        running = jnp.exp(block_total[number])[:, None, None] * running + local_state[number]
    carried_bf = jnp.stack(carried).astype(jnp.bfloat16)
    inter = jnp.exp(cumulative)[..., None] * jnp.einsum(
        "btn,bhpn->bthp", query_blk, carried_bf, preferred_element_type=jnp.float32
    )
    ssd_out = inner_part + inter + skip_gain[None, None, :, None] * signal_blk
    ssd_out = ssd_out.reshape(local_tokens, inner_width)
    gated_out = ssd_out * jax.nn.silu(gate_input.astype(jnp.float32))
    squares = lax.psum(jnp.sum(gated_out * gated_out, axis=1), "mp")
    scaling = 1.0 / jnp.sqrt(squares / INNER + 1e-05)
    gained = (gated_out * norm_gain[None, :]).astype(jnp.bfloat16)
    result = lax.psum_scatter(
        lax.dot_general(
            out_weight, gained, (((0,), (1,)), ((), ())), preferred_element_type=jnp.float32
        ).astype(jnp.bfloat16),
        "mp",
        scatter_dimension=0,
        tiled=True,
    ).astype(jnp.float32)
    mixed_out = (jnp.transpose(result) * scaling[:, None]).astype(jnp.bfloat16)
    return mixed_out


def solution(mesh):
    placed = (
        P("seq", "mp"),
        P("seq", "mp"),
        P("seq", None),
        P("seq", None),
        P("seq", "mp"),
        P("seq", "mp"),
        P("mp"),
        P("mp"),
        P("mp", None),
    )
    return jax.shard_map(
        on_device, mesh=mesh, in_specs=placed, out_specs=P("seq", "mp"), check_vma=False
    )
```

profile of v0, /device:TPU:22, one launch (start us, length us, event | category | flops | bytes accessed | tf_op | source)
XLA Modules:
  0.0 226.3 jit_solution(7299658083734155582)
XLA Ops:
  6.5 0.0 copy-start
  6.5 0.0 reduce-scatter.2.cloned.1.call-start
  6.6 0.8 copy_bitcast_fusion.1
  7.4 1.1 reduce-window.6
  8.5 0.2 slice_reduce_fusion
  8.7 0.1 copy_bitcast_fusion
  8.8 0.2 fusion.29
  9.0 0.2 slice_reduce_fusion.2
  9.2 0.8 reshape.87
  10.0 2.3 %copy.33 = bf16[512,1024]{0,1:T(8,128)(2,1)} copy(bf16[512,1024]{1,0:T(8,128)(2,1)} %param.12) | data formatting | bytes 2097152 | tf_op args[1]
  12.3 2.9 %reshape.92 = bf16[2,256,16,64]{3,2,1,0:T(8,128)(2,1)S(1)} reshape(bf16[512,1024]{1,0:T(8,128)(2,1)} %param.11) | data formatting | bytes 2097152 | tf_op jit(solution)/shard_map/reshape | solution.py:33
  15.3 0.0 copy-start.4
  15.3 0.0 copy-start.3
  15.3 2.5 %copy.29 = bf16[2,256,16,64]{1,3,2,0:T(8,128)(2,1)} copy(bf16[2,256,16,64]{3,2,1,0:T(8,128)(2,1)S(1)} %reshape.92) | data formatting | bytes 2097152 | tf_op jit(solution)/shard_map/reshape | solution.py:33
  17.8 0.0 copy-done.4
  17.8 0.1 bitcast_exponential_fusion
  17.9 0.0 copy-done.3
  17.9 1.7 fusion.18
  19.6 0.1 fusion.22
  19.7 23.7 %while.13 = (s32[]{:T(128)}, f32[16,64,128]{2,1,0:T(8,128)S(1)}, f32[16,1,1]{0,2,1:T(1,128)S(1)}, f32[16,64,128]{2,1,0:T(8,128)S(1)}, s32[]{:T(128)}, /*index=5*/s32[]{:T(128)}) while((s32[]{:T(128)}, f32[16,64,128]{2,1,0:T(8,128)S(1)}, f32[16,1,1]{0,2,1:T(1,128)S(1)}, f32[16,64,128]{2,1,0:T(8,128)S(1)}, s32[]{:T(128)}, ...), condition=%wide.region_4.5_spmd.clone, body=%wide.region_3.4_spmd.clone.sunk | while | flops 655363 | bytes 3145911 | solution.py:67
  19.7 0.1 fusion.42
  19.9 1.9 collective-permute-start
  21.8 5.8 %collective-permute-done = bf16[16,64,128]{2,1,0:T(8,128)(2,1)S(1)} collective-permute-done((bf16[16,64,128]{2,1,0:T(8,128)(2,1)S(1)}, bf16[16,64,128]{2,1,0:T(8,128)(2,1)S(1)}, u32[]{:S(2)}, u32[]{:S(2)}) %collective-permute-start) | collective-permute-done | bytes 262176 | tf_op jit(solution)/shard_map/while/body/eval_jaxpr/ppermute | solution.py:13
  27.6 0.1 fusion.42
  27.8 1.9 collective-permute-start
  29.7 5.8 %collective-permute-done = bf16[16,64,128]{2,1,0:T(8,128)(2,1)S(1)} collective-permute-done((bf16[16,64,128]{2,1,0:T(8,128)(2,1)S(1)}, bf16[16,64,128]{2,1,0:T(8,128)(2,1)S(1)}, u32[]{:S(2)}, u32[]{:S(2)}) %collective-permute-start) | collective-permute-done | bytes 262176 | tf_op jit(solution)/shard_map/while/body/eval_jaxpr/ppermute | solution.py:13
  35.5 0.1 fusion.42
  35.7 1.9 collective-permute-start
  37.6 5.8 %collective-permute-done = bf16[16,64,128]{2,1,0:T(8,128)(2,1)S(1)} collective-permute-done((bf16[16,64,128]{2,1,0:T(8,128)(2,1)S(1)}, bf16[16,64,128]{2,1,0:T(8,128)(2,1)S(1)}, u32[]{:S(2)}, u32[]{:S(2)}) %collective-permute-start) | collective-permute-done | bytes 262176 | tf_op jit(solution)/shard_map/while/body/eval_jaxpr/ppermute | solution.py:13
  43.4 0.1 convert_bitcast_fusion
  43.5 0.0 copy-start.1
  43.6 0.0 copy-start.6
  43.6 0.2 fusion.34
  43.8 0.4 fusion.23
  44.2 0.5 copy-done.1
  44.8 0.0 copy-done.6
  44.8 2.6 %fusion.11 = f32[2,256,16,64]{1,3,2,0:T(8,128)S(1)} fusion(bf16[2,256,16,64]{1,3,2,0:T(8,128)(2,1)S(1)} %copy-done.1, f32[2,16,64,256]{3,2,1,0:T(8,128)S(1)} %fusion.23, f32[2,16,256]{2,1,0:T(8,128)S(1)} %copy.27, f32[2,16,256]{2,1,0:T(8,128)S(1)} %get-tuple-element.87, f32[2,256,256]{2,1,0:T(8,128)S(1)} %fusion.34, ...), kind=kOutput, calls=%fused_computation.18 | convolution fusion | flops 281542656 | bytes 5931072 | tf_op jit(solution)/shard_map/bhts,bshp->bthp/dot_general | solution.py:47
  47.3 1.6 copy.32
  49.0 0.0 copy-start.5
  49.0 0.2 copy.42
  49.2 1.0 copy-done.2
  50.2 0.0 copy-done.5
  50.2 17.3 %fusion.2 = bf16[8192,512]{0,1:T(8,128)(2,1)} fusion(bf16[1024,8192]{1,0:T(8,128)(2,1)} %param.19, f32[1024]{0:T(1024)S(1)} %copy-done.5, f32[512,1024]{0,1:T(8,128)S(1)} %bitcast.88, bf16[512,1024]{0,1:T(8,128)(2,1)S(1)} %copy-done.2), kind=kOutput, calls=%fused_computation.4 | convolution fusion | flops 8598323200 | bytes 28315648 | tf_op jit(solution)/shard_map/dot_general | solution.py:84
  67.5 0.0 reduce-scatter.2.cloned.1.call-update
  67.6 0.7 multiply_reduce_fusion
  68.2 15.3 %psum.7 = f32[512]{0:T(512)S(1)} all-reduce(f32[512]{0:T(512)S(1)} %multiply_reduce_fusion), channel_id=1, replica_groups=mesh['seq'=4,'mp'=8] {'mp'}, use_global_device_ids=true, to_apply=%region_7.8 | all-reduce | flops 512 | bytes 4096 | tf_op jit(solution)/shard_map/psum | solution.py:80
  83.5 133.5 %reduce-scatter.2.cloned.1.call-done = bf16[1024,512]{0,1:T(8,128)(2,1)} async-done(((bf16[8192,512]{0,1:T(8,128)(2,1)}), bf16[1024,512]{0,1:T(8,128)(2,1)}) %reduce-scatter.2.cloned.1.call-update) | async-done | bytes 1048592 | tf_op jit(solution)/shard_map/reduce_scatter | solution.py:83
  217.0 2.4 %fusion.17 = bf16[512,1024]{1,0:T(8,128)(2,1)} fusion(bf16[1024,512]{0,1:T(8,128)(2,1)} %reduce-scatter.2.cloned.1.call-done, f32[512]{0:T(512)S(1)} %add_rsqrt_fusion), kind=kLoop, calls=%fused_computation.28 | loop fusion | flops 1572864 | bytes 2099200 | tf_op jit(solution)/shard_map/convert_element_type | solution.py:91
  (13 shorter events, 0.2 us)
Async XLA Ops:
  6.5 37.0 %copy-start = (bf16[512,128]{1,0:T(8,128)(2,1)S(1)}, bf16[512,128]{1,0:T(8,128)(2,1)}, u32[]{:S(2)}) copy-start(bf16[512,128]{1,0:T(8,128)(2,1)} %param.14) | copy-start | bytes 393220
  6.5 210.5 %reduce-scatter.2.cloned.1.call-start = ((), (), s32[]{:S(2)}) async-start(), calls=%async_computation.1 | async-start | bytes 9437184 | tf_op jit(solution)/shard_map/reduce_scatter | solution.py:83
  15.3 2.5 %copy-start.4 = (f32[512,16]{0,1:T(8,128)S(1)}, f32[512,16]{0,1:T(8,128)}, u32[]{:S(2)}) copy-start(f32[512,16]{0,1:T(8,128)} %param.16) | copy-start | bytes 98308
  15.3 2.6 %copy-start.3 = (bf16[512,128]{1,0:T(8,128)(2,1)S(1)}, bf16[512,128]{1,0:T(8,128)(2,1)}, u32[]{:S(2)}) copy-start(bf16[512,128]{1,0:T(8,128)(2,1)} %param.13) | copy-start | bytes 393220
  19.9 7.7 %collective-permute-start = (bf16[16,64,128]{2,1,0:T(8,128)(2,1)S(1)}, bf16[16,64,128]{2,1,0:T(8,128)(2,1)S(1)}, u32[]{:S(2)}, u32[]{:S(2)}) collective-permute-start(bf16[16,64,128]{2,1,0:T(8,128)(2,1)S(1)} %fusion.42), channel_id=1, source_target_pairs={{0,8},{8,16},{16,24},{1,9},{9,17},{17,25},{2,10},{10,18},{18,26},{... | collective-permute-start | bytes 786440 | tf_op jit(solution)/shard_map/while/body/eval_jaxpr/ppermute | solution.py:13
  27.8 7.7 %collective-permute-start = (bf16[16,64,128]{2,1,0:T(8,128)(2,1)S(1)}, bf16[16,64,128]{2,1,0:T(8,128)(2,1)S(1)}, u32[]{:S(2)}, u32[]{:S(2)}) collective-permute-start(bf16[16,64,128]{2,1,0:T(8,128)(2,1)S(1)} %fusion.42), channel_id=1, source_target_pairs={{0,8},{8,16},{16,24},{1,9},{9,17},{17,25},{2,10},{10,18},{18,26},{... | collective-permute-start | bytes 786440 | tf_op jit(solution)/shard_map/while/body/eval_jaxpr/ppermute | solution.py:13
  35.7 7.7 %collective-permute-start = (bf16[16,64,128]{2,1,0:T(8,128)(2,1)S(1)}, bf16[16,64,128]{2,1,0:T(8,128)(2,1)S(1)}, u32[]{:S(2)}, u32[]{:S(2)}) collective-permute-start(bf16[16,64,128]{2,1,0:T(8,128)(2,1)S(1)} %fusion.42), channel_id=1, source_target_pairs={{0,8},{8,16},{16,24},{1,9},{9,17},{17,25},{2,10},{10,18},{18,26},{... | collective-permute-start | bytes 786440 | tf_op jit(solution)/shard_map/while/body/eval_jaxpr/ppermute | solution.py:13
  43.5 1.2 copy-start.1
  43.6 1.2 copy-start.6
  49.0 1.2 copy-start.2
  49.0 1.2 copy-start.5
Sparse Core Ops, SparseCore 0:
  67.7 149.2 reduce-scatter.1
where the time goes:
time: 230 us; the launch traced here: 226 us
  waiting for transfers between devices  151 us (66%)
  matrix products  22.2 us (10%)
  blocking collectives  15.3 us (7%)
  between operations  13.6 us (6%)
  local copies, waits for them, and re-layouts  13.1 us (6%)
  starting transfers between devices  5.76 us (3%)
  other arithmetic  5.48 us (2%)
    reduce_scatter x1, waiting for transfers between devices, on_device(): lax.psum_scatter(lax.dot_general(out_weight, gained, (((0,), (1,)), ((),...  133 us
    dot_general x1, matrix products, on_device(): lax.dot_general(out_weight, gained, (((0,), (1,)), ((), ())), preferred_e...  17.3 us
    ppermute x3, waiting for transfers between devices, from_behind(): lax.ppermute(value, axis, [(source, source + steps) for source in range(l...  17.3 us
    psum x1, blocking collectives, on_device(): squares = lax.psum(jnp.sum(gated_out * gated_out, axis=1), 'mp')  15.3 us
    ppermute x3, starting transfers between devices, from_behind(): lax.ppermute(value, axis, [(source, source + steps) for source in range(l...  5.76 us
    reshape x2, local copies, waits for them, and re-layouts, on_device(): signal_blk = signal.reshape(block_count, BLOCK, heads_here, head_width)  5.44 us
  transfers between devices with their start and end apart: 4, of which 4 were waited for; matrix products, arithmetic and copies ran while one was open for 0% of the time, Pallas kernels for 0%

commit v1 on v0

--- a/solution.py
+++ b/solution.py
@@ -1,10 +1,12 @@
 import jax
 import jax.numpy as jnp
 from jax import lax
+from jax.experimental import pallas as pl
+from jax.experimental.pallas import tpu as pltpu
 from jax.sharding import PartitionSpec as P
 
 BLOCK = 256
-INNER = 8192
+MESH = pl.DeviceIdType.MESH
 
 
 def from_behind(value, axis, steps):
@@ -77,19 +79,255 @@
     ssd_out = inner_part + inter + skip_gain[None, None, :, None] * signal_blk
     ssd_out = ssd_out.reshape(local_tokens, inner_width)
     gated_out = ssd_out * jax.nn.silu(gate_input.astype(jnp.float32))
-    squares = lax.psum(jnp.sum(gated_out * gated_out, axis=1), "mp")
-    scaling = 1.0 / jnp.sqrt(squares / INNER + 1e-05)
+    squares = jnp.sum(gated_out * gated_out, axis=1)
     gained = (gated_out * norm_gain[None, :]).astype(jnp.bfloat16)
-    result = lax.psum_scatter(
-        lax.dot_general(
-            out_weight, gained, (((0,), (1,)), ((), ())), preferred_element_type=jnp.float32
-        ).astype(jnp.bfloat16),
-        "mp",
-        scatter_dimension=0,
-        tiled=True,
-    ).astype(jnp.float32)
-    mixed_out = (jnp.transpose(result) * scaling[:, None]).astype(jnp.bfloat16)
-    return mixed_out
+    return project(gained, jnp.broadcast_to(squares[None], (8, local_tokens)), out_weight)
+
+
+PAIRS = 2
+CHUNKS = 4
+
+
+def step_target(step, zm, lines):
+    up = zm // (lines // 2)
+    near = zm * (1 - up) + (lines - 1 - zm) * up
+    if step == lines - 1:
+        return zm
+    turned = (step + near) // (lines - 1)
+    seen = (lines - 1 - step) * (1 - turned) + (step - (lines - 1 - near)) * turned
+    return seen * (1 - up) + (lines - 1 - seen) * up
+
+
+def project_kernel(
+    gained_ref,
+    squares_ref,
+    weight_ref,
+    out_ref,
+    wbuf,
+    peer_out,
+    peer_in,
+    own,
+    from_low,
+    from_high,
+    total,
+    sq_in,
+    w_sem,
+    y_send,
+    y_recv,
+    z_send,
+    low_recv,
+    high_recv,
+    sq_send,
+    sq_recv,
+):
+    me = lax.axis_index("mp")
+    lines = own.shape[0]
+    count = lines * PAIRS
+    zm = me // PAIRS
+    ym = me % PAIRS
+    tokens = gained_ref.shape[0]
+    width = out_ref.shape[1]
+    rows = tokens // CHUNKS
+    tile = min(256, width)
+
+    barrier = pltpu.get_barrier_semaphore()
+    for d in range(1, count):
+        pl.semaphore_signal(
+            barrier, inc=1, device_id={"mp": (me + d) % count}, device_id_type=MESH
+        )
+
+    targets = [step_target(s, zm, lines) for s in range(lines)]
+    columns = [z * PAIRS + 1 - ym for z in targets] + [z * PAIRS + ym for z in targets]
+
+    def w_copy(t):
+        cols = pl.ds(pl.multiple_of(columns[t] * width, width), width)
+        return pltpu.make_async_copy(weight_ref.at[:, cols], wbuf.at[t], w_sem.at[t])
+
+    for t in range(2 * lines):
+        w_copy(t).start()
+
+    def multiply(t, dest, slot):
+        w_copy(t).wait()
+
+        @pl.loop(0, width // tile)
+        def _(i):
+            cols = pl.ds(pl.multiple_of(i * tile, tile), tile)
+            dest[slot, :, cols] = jnp.dot(
+                gained_ref[...], wbuf[t, :, cols], preferred_element_type=jnp.float32
+            ).astype(jnp.bfloat16)
+
+    def y_copy(s, c):
+        part = pl.ds(c * rows, rows)
+        return pltpu.make_async_remote_copy(
+            src_ref=peer_out.at[s, part],
+            dst_ref=peer_in.at[s, part],
+            send_sem=y_send.at[s, c],
+            recv_sem=y_recv.at[s, c],
+            device_id={"mp": zm * PAIRS + 1 - ym},
+            device_id_type=MESH,
+        )
+
+    def sq_copy(d):
+        return pltpu.make_async_remote_copy(
+            src_ref=squares_ref,
+            dst_ref=sq_in.at[me],
+            send_sem=sq_send.at[d],
+            recv_sem=sq_recv.at[me],
+            device_id={"mp": (me + d) % count},
+            device_id_type=MESH,
+        )
+
+    def sq_arrival(source):
+        return pltpu.make_async_remote_copy(
+            src_ref=squares_ref,
+            dst_ref=sq_in.at[source],
+            send_sem=sq_send.at[0],
+            recv_sem=sq_recv.at[source],
+            device_id={"mp": source},
+            device_id_type=MESH,
+        )
+
+    def z_copy(s, c, way):
+        part = pl.ds(c * rows, rows)
+        dest, sems = (from_low, low_recv) if way > 0 else (from_high, high_recv)
+        z = targets[s]
+        return pltpu.make_async_remote_copy(
+            src_ref=own.at[s, part],
+            dst_ref=dest.at[z, part],
+            send_sem=z_send.at[s, c],
+            recv_sem=sems.at[z, c],
+            device_id={"mp": (zm + way) * PAIRS + ym},
+            device_id_type=MESH,
+        )
+
+    for s in range(lines):
+        multiply(s, peer_out, s)
+        if s == 0:
+            pl.semaphore_wait(barrier, count - 1)
+        for c in range(CHUNKS):
+            y_copy(s, c).start()
+        if s == 0:
+            for d in range(1, count):
+                sq_copy(d).start()
+    for s in range(lines):
+        multiply(lines + s, own, s)
+
+    squares = squares_ref[...]
+    for d in range(1, count):
+        source = (me + d) % count
+        sq_arrival(source).wait_recv()
+        squares = squares + sq_in[source]
+    inverse = 1.0 / jnp.sqrt(squares[0:1] / (count * gained_ref.shape[1]) + 1e-05)
+    scaling = jnp.transpose(jnp.broadcast_to(inverse, (128, tokens)))
+
+    for s in range(lines):
+        z = targets[s]
+        for c in range(CHUNKS):
+            part = pl.ds(c * rows, rows)
+            y_copy(s, c).wait_recv()
+            total[...] = own[s, part, :].astype(jnp.float32) + peer_in[s, part, :].astype(
+                jnp.float32
+            )
+
+            @pl.when(jnp.logical_and(z >= zm, zm > 0))
+            def _():
+                z_copy_in(z, c, from_low, low_recv, own, z_send, rows, zm - 1, ym).wait_recv()
+                total[...] += from_low[z, part, :].astype(jnp.float32)
+
+            @pl.when(jnp.logical_and(z <= zm, zm < lines - 1))
+            def _():
+                z_copy_in(z, c, from_high, high_recv, own, z_send, rows, zm + 1, ym).wait_recv()
+                total[...] += from_high[z, part, :].astype(jnp.float32)
+
+            if s < lines - 1:
+                own[s, part, :] = total[...].astype(jnp.bfloat16)
+
+                @pl.when(z > zm)
+                def _():
+                    z_copy(s, c, 1).start()
+
+                @pl.when(z < zm)
+                def _():
+                    z_copy(s, c, -1).start()
+            else:
+                factor = scaling[c * rows : (c + 1) * rows]
+                for k in range(width // 128):
+                    cols = slice(k * 128, (k + 1) * 128)
+                    out_ref[part, cols] = (total[:, cols] * factor).astype(jnp.bfloat16)
+
+    for d in range(1, count):
+        sq_copy(d).wait_send()
+    for s in range(lines):
+        z = targets[s]
+        for c in range(CHUNKS):
+            y_copy(s, c).wait_send()
+            if s < lines - 1:
+
+                @pl.when(z > zm)
+                def _():
+                    z_copy(s, c, 1).wait_send()
+
+                @pl.when(z < zm)
+                def _():
+                    z_copy(s, c, -1).wait_send()
+
+
+def z_copy_in(z, c, dest, sems, own, z_send, rows, near, ym):
+    part = pl.ds(c * rows, rows)
+    return pltpu.make_async_remote_copy(
+        src_ref=own.at[0, part],
+        dst_ref=dest.at[z, part],
+        send_sem=z_send.at[0, c],
+        recv_sem=sems.at[z, c],
+        device_id={"mp": near * PAIRS + ym},
+        device_id_type=MESH,
+    )
+
+
+def project(gained, squares, weight):
+    tokens, depth = gained.shape
+    count = lax.axis_size("mp")
+    lines = count // PAIRS
+    width = weight.shape[1] // count
+    dma = pltpu.SemaphoreType.DMA
+    block = lambda n: pltpu.VMEM((n, tokens, width), jnp.bfloat16)
+    return pl.pallas_call(
+        project_kernel,
+        out_shape=jax.ShapeDtypeStruct((tokens, width), jnp.bfloat16),
+        in_specs=[
+            pl.BlockSpec(memory_space=pltpu.VMEM),
+            pl.BlockSpec(memory_space=pltpu.VMEM),
+            pl.BlockSpec(memory_space=pl.ANY),
+        ],
+        out_specs=pl.BlockSpec(memory_space=pltpu.VMEM),
+        scratch_shapes=[
+            pltpu.VMEM((2 * lines, depth, width), jnp.bfloat16),
+            block(lines),
+            block(lines),
+            block(lines),
+            block(lines),
+            block(lines),
+            pltpu.VMEM((tokens // CHUNKS, width), jnp.float32),
+            pltpu.VMEM((count, 8, tokens), jnp.float32),
+            dma((2 * lines,)),
+            dma((lines, CHUNKS)),
+            dma((lines, CHUNKS)),
+            dma((lines, CHUNKS)),
+            dma((lines, CHUNKS)),
+            dma((lines, CHUNKS)),
+            dma((count,)),
+            dma((count,)),
+        ],
+        compiler_params=pltpu.CompilerParams(
+            collective_id=0, has_side_effects=True, vmem_limit_bytes=56 << 20
+        ),
+        cost_estimate=pl.CostEstimate(
+            flops=2 * tokens * depth * width * count,
+            bytes_accessed=2 * depth * width * count,
+            transcendentals=0,
+        ),
+        name="project",
+    )(gained, squares, weight)
 
 
 def solution(mesh):

time: 230 us -> 152 us (0.66)
  waiting for transfers between devices: 151 us -> 17.3 us
  Pallas kernels: 0 us -> 95.2 us
  matrix products: 22.2 us -> 5.76 us
  blocking collectives: 15.3 us -> 0 us
  between operations: 13.6 us -> 0.16 us
  local copies, waits for them, and re-layouts: 13.1 us -> 19.7 us
    reduce_scatter x1 -> x0, waiting for transfers between devices: 133 us -> none  [on_device(): lax.psum_scatter(lax.dot_general(out_weight, gained, (((0,), (1,)), ((),...]
    pallas_call x0 -> x1, Pallas kernels: none -> 95.2 us  [project(): pl.pallas_call(project_kernel, out_shape=jax.ShapeDtypeStruct((tokens, wi...]
    dot_general x1 -> x0, matrix products: 17.3 us -> none  [on_device(): lax.dot_general(out_weight, gained, (((0,), (1,)), ((), ())), preferred_e...]
    psum x1 -> x0, blocking collectives: 15.3 us -> none  [on_device(): squares = lax.psum(jnp.sum(gated_out * gated_out, axis=1), 'mp')]
    reshape x1 -> x3, local copies, waits for them, and re-layouts: 0.79 us -> 8.1 us  [the longest x2 7.34 us: on_device(): ssd_out = ssd_out.reshape(local_tokens, inner_width)]
    convert_element_type x1 -> x0, other arithmetic: 2.43 us -> none  [on_device(): mixed_out = (jnp.transpose(result) * scaling[:, None]).astype(jnp.bfloat16)]
  transfers between devices with their start and end apart: 4 -> 3, of which waited for: 4 -> 3; matrix products, arithmetic and copies ran while one was open for 0% -> 0% of each run, Pallas kernels for 0% -> 0%
where the time goes in v1:
time: 152 us; the launch traced here: 149 us
  Pallas kernels  95.2 us (63%)
  local copies, waits for them, and re-layouts  19.7 us (13%)
  waiting for transfers between devices  17.3 us (11%)
  matrix products  5.76 us (4%)
  starting transfers between devices  5.76 us (4%)
  other arithmetic  5.5 us (4%)
    pallas_call x1, Pallas kernels, project(): pl.pallas_call(project_kernel, out_shape=jax.ShapeDtypeStruct((tokens, wi...  95.2 us
    ppermute x3, waiting for transfers between devices, from_behind(): lax.ppermute(value, axis, [(source, source + steps) for source in range(l...  17.3 us
    reshape x2, local copies, waits for them, and re-layouts, on_device(): ssd_out = ssd_out.reshape(local_tokens, inner_width)  7.34 us
    ppermute x3, starting transfers between devices, from_behind(): lax.ppermute(value, axis, [(source, source + steps) for source in range(l...  5.76 us
    reshape x2, local copies, waits for them, and re-layouts, on_device(): signal_blk = signal.reshape(block_count, BLOCK, heads_here, head_width)  5.45 us
    unnamed x17, local copies, waits for them, and re-layouts  3.81 us
  transfers between devices with their start and end apart: 3, of which 3 were waited for; matrix products, arithmetic and copies ran while one was open for 0% of the time, Pallas kernels for 0%

profile of v1, /device:TPU:22, one launch (start us, length us, event | category | flops | bytes accessed | tf_op | source)
XLA Modules:
  0.0 149.5 jit_solution(13081733108375393878)
XLA Ops:
  0.0 0.0 copy-start
  0.0 0.9 copy-done
  0.9 0.8 copy_bitcast_fusion.1
  1.7 1.1 reduce-window.6
  2.8 0.2 slice_reduce_fusion
  3.0 0.8 reshape.87
  3.8 0.6 copy.28
  4.4 0.1 copy_bitcast_fusion
  4.5 0.2 fusion.26
  4.7 0.2 slice_reduce_fusion.2
  4.9 1.5 bitcast_exponential_fusion
  6.4 1.1 fusion.30
  7.5 3.0 %reshape.93 = bf16[2,256,16,64]{3,2,1,0:T(8,128)(2,1)S(1)} reshape(bf16[512,1024]{1,0:T(8,128)(2,1)} %param.11) | data formatting | bytes 2097152 | tf_op jit(solution)/shard_map/reshape | solution.py:35
  10.5 0.0 copy-start.3
  10.5 2.5 %copy.30 = bf16[2,256,16,64]{1,3,2,0:T(8,128)(2,1)} copy(bf16[2,256,16,64]{3,2,1,0:T(8,128)(2,1)S(1)} %reshape.93) | data formatting | bytes 2097152 | tf_op jit(solution)/shard_map/reshape | solution.py:35
  13.0 0.0 copy-done.3
  13.0 1.7 %fusion.16 = f32[2,16,64,128]{3,2,1,0:T(8,128)S(1)} fusion(bf16[2,256,128,1]{2,1,3,0:T(8,128)(2,1)S(1)} %bitcast.81, bf16[2,256,16,64]{1,3,2,0:T(8,128)(2,1)} %copy.30, f32[2,256,16]{1,2,0:T(8,128)S(1)} %get-tuple-element.88), kind=kOutput, calls=%fused_computation.25 | convolution fusion | flops 135790592 | bytes 2260992 | tf_op jit(solution)/shard_map/bshp,bsn->bhpn/dot_general | solution.py:55
  14.7 0.1 fusion.19
  14.8 23.7 %while.13 = (s32[]{:T(128)}, f32[16,64,128]{2,1,0:T(8,128)S(1)}, f32[16,1,1]{0,2,1:T(1,128)S(1)}, f32[16,64,128]{2,1,0:T(8,128)S(1)}, s32[]{:T(128)}, /*index=5*/s32[]{:T(128)}) while((s32[]{:T(128)}, f32[16,64,128]{2,1,0:T(8,128)S(1)}, f32[16,1,1]{0,2,1:T(1,128)S(1)}, f32[16,64,128]{2,1,0:T(8,128)S(1)}, s32[]{:T(128)}, ...), condition=%wide.region_4.5_spmd.clone, body=%wide.region_3.4_spmd.clone.sunk | while | flops 655363 | bytes 3145911 | solution.py:69
  14.8 0.1 fusion.37
  15.0 1.9 %collective-permute-start = (bf16[16,64,128]{2,1,0:T(8,128)(2,1)S(1)}, bf16[16,64,128]{2,1,0:T(8,128)(2,1)S(1)}, u32[]{:S(2)}, u32[]{:S(2)}) collective-permute-start(bf16[16,64,128]{2,1,0:T(8,128)(2,1)S(1)} %fusion.37), channel_id=1, source_target_pairs={{0,8},{8,16},{16,24},{1,9},{9,17},{17,25},{2,10},{10,18},{18,26},{... | collective-permute-start | bytes 786440 | tf_op jit(solution)/shard_map/while/body/eval_jaxpr/ppermute | solution.py:15
  16.9 5.8 %collective-permute-done = bf16[16,64,128]{2,1,0:T(8,128)(2,1)S(1)} collective-permute-done((bf16[16,64,128]{2,1,0:T(8,128)(2,1)S(1)}, bf16[16,64,128]{2,1,0:T(8,128)(2,1)S(1)}, u32[]{:S(2)}, u32[]{:S(2)}) %collective-permute-start) | collective-permute-done | bytes 262176 | tf_op jit(solution)/shard_map/while/body/eval_jaxpr/ppermute | solution.py:15
  22.7 0.1 fusion.37
  22.9 1.9 %collective-permute-start = (bf16[16,64,128]{2,1,0:T(8,128)(2,1)S(1)}, bf16[16,64,128]{2,1,0:T(8,128)(2,1)S(1)}, u32[]{:S(2)}, u32[]{:S(2)}) collective-permute-start(bf16[16,64,128]{2,1,0:T(8,128)(2,1)S(1)} %fusion.37), channel_id=1, source_target_pairs={{0,8},{8,16},{16,24},{1,9},{9,17},{17,25},{2,10},{10,18},{18,26},{... | collective-permute-start | bytes 786440 | tf_op jit(solution)/shard_map/while/body/eval_jaxpr/ppermute | solution.py:15
  24.8 5.8 %collective-permute-done = bf16[16,64,128]{2,1,0:T(8,128)(2,1)S(1)} collective-permute-done((bf16[16,64,128]{2,1,0:T(8,128)(2,1)S(1)}, bf16[16,64,128]{2,1,0:T(8,128)(2,1)S(1)}, u32[]{:S(2)}, u32[]{:S(2)}) %collective-permute-start) | collective-permute-done | bytes 262176 | tf_op jit(solution)/shard_map/while/body/eval_jaxpr/ppermute | solution.py:15
  30.6 0.1 fusion.37
  30.7 1.9 %collective-permute-start = (bf16[16,64,128]{2,1,0:T(8,128)(2,1)S(1)}, bf16[16,64,128]{2,1,0:T(8,128)(2,1)S(1)}, u32[]{:S(2)}, u32[]{:S(2)}) collective-permute-start(bf16[16,64,128]{2,1,0:T(8,128)(2,1)S(1)} %fusion.37), channel_id=1, source_target_pairs={{0,8},{8,16},{16,24},{1,9},{9,17},{17,25},{2,10},{10,18},{18,26},{... | collective-permute-start | bytes 786440 | tf_op jit(solution)/shard_map/while/body/eval_jaxpr/ppermute | solution.py:15
  32.7 5.8 %collective-permute-done = bf16[16,64,128]{2,1,0:T(8,128)(2,1)S(1)} collective-permute-done((bf16[16,64,128]{2,1,0:T(8,128)(2,1)S(1)}, bf16[16,64,128]{2,1,0:T(8,128)(2,1)S(1)}, u32[]{:S(2)}, u32[]{:S(2)}) %collective-permute-start) | collective-permute-done | bytes 262176 | tf_op jit(solution)/shard_map/while/body/eval_jaxpr/ppermute | solution.py:15
  38.5 0.0 copy-start.1
  38.5 0.0 copy-start.4
  38.5 0.0 copy-start.5
  38.5 0.0 copy-start.7
  38.5 0.1 convert_bitcast_fusion
  38.7 0.4 fusion.20
  39.1 0.6 copy-done.1
  39.7 0.0 copy-done.4
  39.7 0.0 copy-done.5
  39.7 0.0 copy-done.7
  39.7 2.5 %fusion.10 = f32[2,256,16,64]{1,3,2,0:T(8,128)S(1)} fusion(bf16[2,256,16,64]{1,3,2,0:T(8,128)(2,1)S(1)} %copy-done.1, f32[2,16,64,256]{3,2,1,0:T(8,128)S(1)} %fusion.20, f32[2,16,256]{2,1,0:T(8,128)S(1)} %copy-done.4, f32[2,16,256]{2,1,0:T(8,128)S(1)} %get-tuple-element.89, f32[2,256,256]{2,1,0:T(8,128)S(1)} %fusion.30, ...), kind=kOutput, calls=%fused_computation.16 | convolution fusion | flops 281542656 | bytes 5931072 | tf_op jit(solution)/shard_map/bhts,bshp->bthp/dot_general | solution.py:49
  42.3 3.8 %copy.37 = f32[2,256,16,64]{3,2,1,0:T(8,128)} copy(f32[2,256,16,64]{1,3,2,0:T(8,128)S(1)} %fusion.10) | data formatting | bytes 4194304 | tf_op jit(solution)/shard_map/reshape | solution.py:80
  46.0 0.0 copy-start.2
  46.0 3.6 %reshape.92 = f32[512,1024]{1,0:T(8,128)S(1)} reshape(f32[2,256,16,64]{3,2,1,0:T(8,128)} %copy.37) | data formatting | bytes 4194304 | tf_op jit(solution)/shard_map/reshape | solution.py:80
  49.6 0.0 copy-done.2
  49.6 0.0 copy-done.6
  49.6 1.8 %multiply_reduce_fusion = (f32[512]{0:T(512)S(1)}, bf16[512,1024]{1,0:T(8,128)(2,1)}) fusion(f32[512,1024]{1,0:T(8,128)S(1)} %reshape.92, bf16[512,1024]{1,0:T(8,128)(2,1)S(1)} %copy-done.2, f32[1024]{0:T(1024)S(1)} %copy-done.6), kind=kLoop, calls=%fused_computation.23 | loop fusion | flops 5242368 | bytes 4200448 | tf_op jit(solution)/shard_map/reduce_sum | solution.py:82
  51.4 0.6 broadcast_in_dim.12.squares_ref
  52.0 95.2 %project.1 = bf16[512,1024]{1,0:T(8,128)(2,1)} custom-call(bf16[512,1024]{1,0:T(8,128)(2,1)} %get-tuple-element.84.gained_ref, f32[8,512]{1,0:T(8,128)} %broadcast_in_dim.12.squares_ref, bf16[1024,8192]{1,0:T(8,128)(2,1)} %weight_ref.1), custom_call_target="tpu_custom_call" | custom-call | flops 8589934592 | bytes 16777216 | tf_op jit(solution)/shard_map/project/pallas_call | solution.py:294
  147.2 2.3 %copy.63 = bf16[512,1024]{1,0:T(8,128)(2,1)} copy(bf16[512,1024]{1,0:T(8,128)(2,1)} %project.1) | data formatting | bytes 2097152
  (10 shorter events, 0.2 us)
Async XLA Ops:
  0.0 0.9 copy-start
  10.5 2.5 %copy-start.3 = (bf16[512,128]{1,0:T(8,128)(2,1)S(1)}, bf16[512,128]{1,0:T(8,128)(2,1)}, u32[]{:S(2)}) copy-start(bf16[512,128]{1,0:T(8,128)(2,1)} %param.13) | copy-start | bytes 393220
  15.0 7.7 %collective-permute-start = (bf16[16,64,128]{2,1,0:T(8,128)(2,1)S(1)}, bf16[16,64,128]{2,1,0:T(8,128)(2,1)S(1)}, u32[]{:S(2)}, u32[]{:S(2)}) collective-permute-start(bf16[16,64,128]{2,1,0:T(8,128)(2,1)S(1)} %fusion.37), channel_id=1, source_target_pairs={{0,8},{8,16},{16,24},{1,9},{9,17},{17,25},{2,10},{10,18},{18,26},{... | collective-permute-start | bytes 786440 | tf_op jit(solution)/shard_map/while/body/eval_jaxpr/ppermute | solution.py:15
  22.9 7.7 %collective-permute-start = (bf16[16,64,128]{2,1,0:T(8,128)(2,1)S(1)}, bf16[16,64,128]{2,1,0:T(8,128)(2,1)S(1)}, u32[]{:S(2)}, u32[]{:S(2)}) collective-permute-start(bf16[16,64,128]{2,1,0:T(8,128)(2,1)S(1)} %fusion.37), channel_id=1, source_target_pairs={{0,8},{8,16},{16,24},{1,9},{9,17},{17,25},{2,10},{10,18},{18,26},{... | collective-permute-start | bytes 786440 | tf_op jit(solution)/shard_map/while/body/eval_jaxpr/ppermute | solution.py:15
  30.7 7.7 %collective-permute-start = (bf16[16,64,128]{2,1,0:T(8,128)(2,1)S(1)}, bf16[16,64,128]{2,1,0:T(8,128)(2,1)S(1)}, u32[]{:S(2)}, u32[]{:S(2)}) collective-permute-start(bf16[16,64,128]{2,1,0:T(8,128)(2,1)S(1)} %fusion.37), channel_id=1, source_target_pairs={{0,8},{8,16},{16,24},{1,9},{9,17},{17,25},{2,10},{10,18},{18,26},{... | collective-permute-start | bytes 786440 | tf_op jit(solution)/shard_map/while/body/eval_jaxpr/ppermute | solution.py:15
  38.5 1.2 copy-start.1
  38.5 1.2 copy-start.4
  38.5 1.2 copy-start.5
  38.5 1.2 copy-start.7
  46.0 3.6 %copy-start.2 = (bf16[512,1024]{1,0:T(8,128)(2,1)S(1)}, bf16[512,1024]{1,0:T(8,128)(2,1)}, u32[]{:S(2)}) copy-start(bf16[512,1024]{1,0:T(8,128)(2,1)} %param.12) | copy-start | bytes 3145732
  46.0 3.6 %copy-start.6 = (f32[1024]{0:T(1024)S(1)}, f32[1024]{0:T(1024)}, u32[]{:S(2)}) copy-start(f32[1024]{0:T(1024)} %param.18) | copy-start | bytes 12292

commit v2 on v1

--- a/solution.py
+++ b/solution.py
@@ -6,86 +6,12 @@
 from jax.sharding import PartitionSpec as P
 
 BLOCK = 256
-MESH = pl.DeviceIdType.MESH
-
-
-def from_behind(value, axis, steps):
-    count = lax.axis_size(axis)
-    leading, last = (max(0, -steps), min(count, count - steps))
-    return lax.ppermute(value, axis, [(source, source + steps) for source in range(leading, last)])
-
-
-def on_device(
-    signal,
-    gate_input,
-    input_map,
-    output_map,
-    log_decay,
-    step_size,
-    skip_gain,
-    norm_gain,
-    out_weight,
-):
-    local_tokens = signal.shape[0]
-    inner_width = signal.shape[1]
-    heads_here = log_decay.shape[1]
-    head_width = inner_width // heads_here
-    state_width = input_map.shape[1]
-    block_count = local_tokens // BLOCK
-    signal_blk = signal.reshape(block_count, BLOCK, heads_here, head_width)
-    keys_blk = input_map.reshape(block_count, BLOCK, state_width)
-    query_blk = output_map.reshape(block_count, BLOCK, state_width)
-    decay_blk = log_decay.reshape(block_count, BLOCK, heads_here)
-    steps_blk = step_size.reshape(block_count, BLOCK, heads_here)
-    cumulative = jnp.cumsum(decay_blk, axis=1)
-    scores = jnp.einsum("btn,bsn->bts", query_blk, keys_blk, preferred_element_type=jnp.float32)
-    cum_heads = jnp.swapaxes(cumulative, 1, 2)
-    log_gaps = cum_heads[:, :, :, None] - cum_heads[:, :, None, :]
-    causal = jnp.arange(BLOCK)[:, None] >= jnp.arange(BLOCK)[None, :]
-    decays = jnp.exp(jnp.where(causal, log_gaps, -jnp.inf))
-    weights = (scores[:, None] * decays * jnp.swapaxes(steps_blk, 1, 2)[:, :, None, :]).astype(
-        jnp.bfloat16
-    )
-    inner_part = jnp.einsum(
-        "bhts,bshp->bthp", weights, signal_blk, preferred_element_type=jnp.float32
-    )
-    feed_rows = (
-        signal_blk * (steps_blk * jnp.exp(cumulative[:, -1:, :] - cumulative))[..., None]
-    ).astype(jnp.bfloat16)
-    local_state = jnp.einsum(
-        "bshp,bsn->bhpn", feed_rows, keys_blk, preferred_element_type=jnp.float32
-    )
-    block_total = cumulative[:, -1, :]
-    dev_total = jnp.sum(block_total, axis=0)
-    running = jnp.zeros((heads_here, head_width, state_width), jnp.float32)
-    for number in range(block_count):
-        running = jnp.exp(block_total[number])[:, None, None] * running + local_state[number]
-    dev_state = running
-
-    def relay_step(number, incoming):
-        outgoing = jnp.exp(dev_total)[:, None, None] * incoming + dev_state
-        return from_behind(outgoing.astype(jnp.bfloat16), "seq", 1).astype(outgoing.dtype)
-
-    incoming = lax.fori_loop(0, lax.axis_size("seq") - 1, relay_step, jnp.zeros_like(dev_state))
-    running = incoming
-    carried = []
-    for number in range(block_count):
-        carried.append(running)
-        running = jnp.exp(block_total[number])[:, None, None] * running + local_state[number]
-    carried_bf = jnp.stack(carried).astype(jnp.bfloat16)
-    inter = jnp.exp(cumulative)[..., None] * jnp.einsum(
-        "btn,bhpn->bthp", query_blk, carried_bf, preferred_element_type=jnp.float32
-    )
-    ssd_out = inner_part + inter + skip_gain[None, None, :, None] * signal_blk
-    ssd_out = ssd_out.reshape(local_tokens, inner_width)
-    gated_out = ssd_out * jax.nn.silu(gate_input.astype(jnp.float32))
-    squares = jnp.sum(gated_out * gated_out, axis=1)
-    gained = (gated_out * norm_gain[None, :]).astype(jnp.bfloat16)
-    return project(gained, jnp.broadcast_to(squares[None], (8, local_tokens)), out_weight)
-
-
 PAIRS = 2
 CHUNKS = 4
+RELAY_CHUNKS = 2
+LANES = 128
+MESH = pl.DeviceIdType.MESH
+EXACT = lax.Precision.HIGHEST
 
 
 def step_target(step, zm, lines):
@@ -98,11 +24,25 @@
     return seen * (1 - up) + (lines - 1 - seen) * up
 
 
-def project_kernel(
+def layer_kernel(
+    signal_ref,
+    gate_ref,
+    keys_ref,
+    query_ref,
+    decay_ref,
+    step_ref,
+    skip_ref,
+    gain_ref,
+    weight_ref,
+    out_ref,
     gained_ref,
     squares_ref,
-    weight_ref,
-    out_ref,
+    inner,
+    local,
+    spread,
+    relay_out,
+    relay_in,
+    square_sum,
     wbuf,
     peer_out,
     peer_in,
@@ -119,6 +59,8 @@
     high_recv,
     sq_send,
     sq_recv,
+    relay_send,
+    relay_recv,
 ):
     me = lax.axis_index("mp")
     lines = own.shape[0]
@@ -136,6 +78,13 @@
             barrier, inc=1, device_id={"mp": (me + d) % count}, device_id_type=MESH
         )
 
+    seq = lax.axis_index("seq")
+    seq_count = lax.axis_size("seq")
+    for d in (1, seq_count - 1):
+        pl.semaphore_signal(
+            barrier, inc=1, device_id={"seq": (seq + d) % seq_count}, device_id_type=MESH
+        )
+
     targets = [step_target(s, zm, lines) for s in range(lines)]
     columns = [z * PAIRS + 1 - ym for z in targets] + [z * PAIRS + ym for z in targets]
 
@@ -145,6 +94,144 @@
 
     for t in range(2 * lines):
         w_copy(t).start()
+
+    heads = decay_ref.shape[0]
+    width_in = signal_ref.shape[1]
+    head_width = width_in // heads
+    state_width = keys_ref.shape[1]
+    blocks = tokens // BLOCK
+    half = BLOCK // 2
+    row_ids = lax.broadcasted_iota(jnp.int32, (BLOCK, BLOCK), 0)
+    col_ids = lax.broadcasted_iota(jnp.int32, (BLOCK, BLOCK), 1)
+    upper = jnp.where(row_ids <= col_ids, 1.0, 0.0).astype(jnp.float32)
+    barred = jnp.where(row_ids >= col_ids, 0.0, -1e30).astype(jnp.float32)
+    low_lane = lax.broadcasted_iota(jnp.int32, (half, LANES), 1) < head_width
+    slot_ids = lax.broadcasted_iota(jnp.int32, (LANES, width_in), 0)
+    head_ids = lax.broadcasted_iota(jnp.int32, (LANES, width_in), 1) // head_width
+    pick_feed = jnp.where(slot_ids == head_ids + heads, 1.0, 0.0).astype(jnp.float32)
+    pick_grow = jnp.where(slot_ids == head_ids + 2 * heads, 1.0, 0.0).astype(jnp.float32)
+
+    cum_rows, cum_cols = [], []
+    for b in range(blocks):
+        span = slice(b * BLOCK, (b + 1) * BLOCK)
+        cum_t = jnp.dot(
+            decay_ref[:, span], upper, precision=EXACT, preferred_element_type=jnp.float32
+        )
+        feed_t = step_ref[:, span] * jnp.exp(cum_t[:, BLOCK - 1 : BLOCK] - cum_t)
+        filler = jnp.zeros((LANES - 3 * heads, BLOCK), jnp.float32)
+        cols = jnp.transpose(jnp.concatenate([cum_t, feed_t, jnp.exp(cum_t), filler], axis=0))
+        cum_rows.append(cum_t)
+        cum_cols.append(cols)
+        feed = jnp.dot(cols, pick_feed, precision=EXACT, preferred_element_type=jnp.float32)
+        spread[span, :] = jnp.dot(
+            cols, pick_grow, precision=EXACT, preferred_element_type=jnp.float32
+        )
+        feed_rows = (signal_ref[span, :].astype(jnp.float32) * feed).astype(jnp.bfloat16)
+        keys_t = jnp.transpose(keys_ref[span, :].astype(jnp.float32)).astype(jnp.bfloat16)
+        local[b] = jnp.dot(keys_t, feed_rows, preferred_element_type=jnp.float32)
+
+    def block_decay(b):
+        last = (b + 1) * BLOCK - 1
+        return spread[last : last + 1, :]
+
+    def relay_copy(c):
+        part = pl.ds(c * (state_width // RELAY_CHUNKS), state_width // RELAY_CHUNKS)
+        return pltpu.make_async_remote_copy(
+            src_ref=relay_out.at[part],
+            dst_ref=relay_in.at[part],
+            send_sem=relay_send.at[c],
+            recv_sem=relay_recv.at[c],
+            device_id={"seq": (seq + 1) % seq_count},
+            device_id_type=MESH,
+        )
+
+    pl.semaphore_wait(barrier, count + 1)
+
+    @pl.when(seq == 0)
+    def _():
+        relay_in[...] = jnp.zeros_like(relay_in)
+
+    def relay():
+        for c in range(RELAY_CHUNKS):
+            n = state_width // RELAY_CHUNKS
+            part = slice(c * n, (c + 1) * n)
+
+            @pl.when(seq > 0)
+            def _():
+                relay_copy(c).wait_recv()
+
+            @pl.when(seq < seq_count - 1)
+            def _():
+                state = relay_in[part, :].astype(jnp.float32)
+                for b in range(blocks):
+                    state = block_decay(b) * state + local[b, part, :]
+                relay_out[part, :] = state.astype(jnp.bfloat16)
+                relay_copy(c).start()
+
+    def inner_pair(b, p, scores):
+        cols = slice(p * LANES, (p + 1) * LANES)
+        base = b * BLOCK
+        signal_pair = signal_ref[base : base + BLOCK, cols]
+        parts = []
+        for top, wide in ((0, half), (half, BLOCK)):
+            outs = []
+            for h in (2 * p, 2 * p + 1):
+                gaps = (
+                    cum_cols[b][top : top + half, h : h + 1]
+                    - cum_rows[b][h : h + 1, :wide]
+                    + barred[top : top + half, :wide]
+                )
+                scaled = scores[top : top + half, :wide] * jnp.exp(gaps)
+                scaled = scaled * step_ref[h : h + 1, base : base + wide]
+                outs.append(
+                    jnp.dot(
+                        scaled.astype(jnp.bfloat16),
+                        signal_pair[:wide],
+                        preferred_element_type=jnp.float32,
+                    )
+                )
+            parts.append(jnp.where(low_lane, outs[0], outs[1]))
+        for number, value in enumerate(parts):
+            at = slice(base + number * half, base + (number + 1) * half)
+            inner[at, cols] = value + skip_ref[:, cols] * signal_ref[at, cols].astype(jnp.float32)
+
+    turn = 0
+    pair_count = width_in // LANES
+    every = max(1, blocks * pair_count // 3)
+    done = 0
+    for b in range(blocks):
+        span = slice(b * BLOCK, (b + 1) * BLOCK)
+        scores = lax.dot_general(
+            query_ref[span, :],
+            keys_ref[span, :],
+            (((1,), (1,)), ((), ())),
+            preferred_element_type=jnp.float32,
+        )
+        for p in range(pair_count):
+            if done % every == 0 and turn < 3:
+                pl.when(seq == turn)(relay)
+                turn += 1
+            inner_pair(b, p, scores)
+            done += 1
+    pl.when(seq >= turn)(relay)
+
+    state = relay_in[...].astype(jnp.float32)
+    for b in range(blocks):
+        span = slice(b * BLOCK, (b + 1) * BLOCK)
+        carried = state.astype(jnp.bfloat16)
+        squared = jnp.zeros((BLOCK, LANES), jnp.float32)
+        for p in range(pair_count):
+            cols = slice(p * LANES, (p + 1) * LANES)
+            read = jnp.dot(query_ref[span, :], carried[:, cols], preferred_element_type=jnp.float32)
+            gate = gate_ref[span, cols].astype(jnp.float32)
+            gated = (inner[span, cols] + spread[span, cols] * read) * (gate / (1.0 + jnp.exp(-gate)))
+            squared = squared + gated * gated
+            gained_ref[span, cols] = (gated * gain_ref[:, cols]).astype(jnp.bfloat16)
+        square_sum[span, :] = squared
+        if b < blocks - 1:
+            state = block_decay(b) * state + local[b]
+    total_row = jnp.sum(jnp.transpose(square_sum[...]), axis=0, keepdims=True)
+    squares_ref[...] = jnp.broadcast_to(total_row, (8, tokens))
 
     def multiply(t, dest, slot):
         w_copy(t).wait()
@@ -202,8 +289,6 @@
 
     for s in range(lines):
         multiply(s, peer_out, s)
-        if s == 0:
-            pl.semaphore_wait(barrier, count - 1)
         for c in range(CHUNKS):
             y_copy(s, c).start()
         if s == 0:
@@ -254,6 +339,11 @@
                 for k in range(width // 128):
                     cols = slice(k * 128, (k + 1) * 128)
                     out_ref[part, cols] = (total[:, cols] * factor).astype(jnp.bfloat16)
+
+    @pl.when(seq < seq_count - 1)
+    def _():
+        for c in range(RELAY_CHUNKS):
+            relay_copy(c).wait_send()
 
     for d in range(1, count):
         sq_copy(d).wait_send()
@@ -284,29 +374,47 @@
     )
 
 
-def project(gained, squares, weight):
-    tokens, depth = gained.shape
+def on_device(
+    signal,
+    gate_input,
+    input_map,
+    output_map,
+    log_decay,
+    step_size,
+    skip_gain,
+    norm_gain,
+    out_weight,
+):
+    tokens, depth = signal.shape
+    heads = log_decay.shape[1]
+    state_width = input_map.shape[1]
     count = lax.axis_size("mp")
     lines = count // PAIRS
-    width = weight.shape[1] // count
+    width = out_weight.shape[1] // count
+    skip_lanes = jnp.repeat(skip_gain, depth // heads)[None]
     dma = pltpu.SemaphoreType.DMA
-    block = lambda n: pltpu.VMEM((n, tokens, width), jnp.bfloat16)
+    held = lambda n: pltpu.VMEM((n, tokens, width), jnp.bfloat16)
+    whole = pl.BlockSpec(memory_space=pltpu.VMEM)
     return pl.pallas_call(
-        project_kernel,
+        layer_kernel,
         out_shape=jax.ShapeDtypeStruct((tokens, width), jnp.bfloat16),
-        in_specs=[
-            pl.BlockSpec(memory_space=pltpu.VMEM),
-            pl.BlockSpec(memory_space=pltpu.VMEM),
-            pl.BlockSpec(memory_space=pl.ANY),
-        ],
-        out_specs=pl.BlockSpec(memory_space=pltpu.VMEM),
+        in_specs=[whole] * 8 + [pl.BlockSpec(memory_space=pl.ANY)],
+        out_specs=whole,
         scratch_shapes=[
+            pltpu.VMEM((tokens, depth), jnp.bfloat16),
+            pltpu.VMEM((8, tokens), jnp.float32),
+            pltpu.VMEM((tokens, depth), jnp.float32),
+            pltpu.VMEM((tokens // BLOCK, state_width, depth), jnp.float32),
+            pltpu.VMEM((tokens, depth), jnp.float32),
+            pltpu.VMEM((state_width, depth), jnp.bfloat16),
+            pltpu.VMEM((state_width, depth), jnp.bfloat16),
+            pltpu.VMEM((tokens, LANES), jnp.float32),
             pltpu.VMEM((2 * lines, depth, width), jnp.bfloat16),
-            block(lines),
-            block(lines),
-            block(lines),
-            block(lines),
-            block(lines),
+            held(lines),
+            held(lines),
+            held(lines),
+            held(lines),
+            held(lines),
             pltpu.VMEM((tokens // CHUNKS, width), jnp.float32),
             pltpu.VMEM((count, 8, tokens), jnp.float32),
             dma((2 * lines,)),
@@ -317,17 +425,24 @@
             dma((lines, CHUNKS)),
             dma((count,)),
             dma((count,)),
+            dma((RELAY_CHUNKS,)),
+            dma((RELAY_CHUNKS,)),
         ],
         compiler_params=pltpu.CompilerParams(
-            collective_id=0, has_side_effects=True, vmem_limit_bytes=56 << 20
+            collective_id=0, has_side_effects=True, vmem_limit_bytes=58 << 20
         ),
-        cost_estimate=pl.CostEstimate(
-            flops=2 * tokens * depth * width * count,
-            bytes_accessed=2 * depth * width * count,
-            transcendentals=0,
-        ),
-        name="project",
-    )(gained, squares, weight)
+        name="layer",
+    )(
+        signal,
+        gate_input,
+        input_map,
+        output_map,
+        jnp.transpose(log_decay),
+        jnp.transpose(step_size),
+        skip_lanes,
+        norm_gain[None],
+        out_weight,
+    )
 
 
 def solution(mesh):

time: 152 us -> 120 us (0.79)
  Pallas kernels: 95.2 us -> 114 us
  waiting for transfers between devices: 17.3 us -> 0 us
  local copies, waits for them, and re-layouts: 19.7 us -> 3.66 us
  matrix products: 5.76 us -> 0 us
  starting transfers between devices: 5.76 us -> 0 us
  other arithmetic: 5.5 us -> 0 us
    pallas_call x1, Pallas kernels: 95.2 us -> 114 us  [on_device(): pl.pallas_call(layer_kernel, out_shape=jax.ShapeDtypeStruct((tokens, widt...]
    ppermute x3 -> x0, waiting for transfers between devices: 17.3 us -> none  [from_behind(): lax.ppermute(value, axis, [(source, source + steps) for source in range(l...]
    reshape x6 -> x0, local copies, waits for them, and re-layouts: 14.3 us -> none  [the longest x2 7.34 us: on_device(): ssd_out = ssd_out.reshape(local_tokens, inner_width)]
    ppermute x3 -> x0, starting transfers between devices: 5.76 us -> none  [from_behind(): lax.ppermute(value, axis, [(source, source + steps) for source in range(l...]
    dot_general x4 -> x0, matrix products: 5.76 us -> none  [the longest x1 2.54 us: on_device(): jnp.einsum('bhts,bshp->bthp', weights, signal_blk, preferred_element_type...]
    reduce_sum x2 -> x0, other arithmetic: 1.97 us -> none  [the longest x1 1.76 us: on_device(): squares = jnp.sum(gated_out * gated_out, axis=1)]
    unnamed x17 -> x1, local copies, waits for them, and re-layouts: 3.81 us -> 2.26 us
  transfers between devices with their start and end apart: 3 -> 0, of which waited for: 3 -> 0; matrix products, arithmetic and copies ran while one was open for 0% -> 0% of each run, Pallas kernels for 0% -> 0%
where the time goes in v2:
time: 120 us; the launch traced here: 118 us
  Pallas kernels  114 us (95%)
  local copies, waits for them, and re-layouts  3.66 us (3%)
    pallas_call x1, Pallas kernels, on_device(): pl.pallas_call(layer_kernel, out_shape=jax.ShapeDtypeStruct((tokens, widt...  114 us

profile of v2, /device:TPU:22, one launch (start us, length us, event | category | flops | bytes accessed | tf_op | source)
XLA Modules:
  0.0 117.6 jit_solution(14517870192780334792)
XLA Ops:
  0.0 0.7 broadcast_in_dim.6
  0.7 0.7 broadcast_in_dim_reshape.3.skip_ref
  1.4 113.9 %layer.1 = bf16[512,1024]{1,0:T(8,128)(2,1)} custom-call(bf16[512,1024]{1,0:T(8,128)(2,1)} %signal_ref.1, bf16[512,1024]{1,0:T(8,128)(2,1)} %gate_ref.1, bf16[512,128]{1,0:T(8,128)(2,1)} %keys_ref.1, bf16[512,128]{1,0:T(8,128)(2,1)} %query_ref.1, f32[16,512]{1,0:T(8,128)} %bitcast.3, f32[16,512]{1,0:T(8,128)} %bitcast.4, ...), custom_call_target="tpu_custom_call" | custom-call | tf_op jit(solution)/shard_map/layer/pallas_call | solution.py:398
  115.3 2.3 %copy.11 = bf16[512,1024]{1,0:T(8,128)(2,1)} copy(bf16[512,1024]{1,0:T(8,128)(2,1)} %layer.1) | data formatting | bytes 2097152

commit v3 on v2

--- a/solution.py
+++ b/solution.py
@@ -9,6 +9,7 @@
 PAIRS = 2
 CHUNKS = 4
 RELAY_CHUNKS = 2
+LINE_SHARE = 8
 LANES = 128
 MESH = pl.DeviceIdType.MESH
 EXACT = lax.Precision.HIGHEST
@@ -43,6 +44,9 @@
     relay_out,
     relay_in,
     square_sum,
+    line_total,
+    line_low,
+    line_high,
     wbuf,
     peer_out,
     peer_in,
@@ -61,6 +65,11 @@
     sq_recv,
     relay_send,
     relay_recv,
+    line_send,
+    line_low_recv,
+    line_high_recv,
+    cross_send,
+    cross_recv,
 ):
     me = lax.axis_index("mp")
     lines = own.shape[0]
@@ -69,7 +78,9 @@
     ym = me % PAIRS
     tokens = gained_ref.shape[0]
     width = out_ref.shape[1]
-    rows = tokens // CHUNKS
+    line_rows = tokens // LINE_SHARE
+    rows = (tokens - line_rows) // CHUNKS
+    line_part = pl.ds(tokens - line_rows, line_rows)
     tile = min(256, width)
 
     barrier = pltpu.get_barrier_semaphore()
@@ -193,7 +204,9 @@
             parts.append(jnp.where(low_lane, outs[0], outs[1]))
         for number, value in enumerate(parts):
             at = slice(base + number * half, base + (number + 1) * half)
-            inner[at, cols] = value + skip_ref[:, cols] * signal_ref[at, cols].astype(jnp.float32)
+            inner[at, cols] = value + jnp.where(
+                low_lane, skip_ref[2 * p], skip_ref[2 * p + 1]
+            ) * signal_ref[at, cols].astype(jnp.float32)
 
     turn = 0
     pair_count = width_in // LANES
@@ -215,6 +228,26 @@
             done += 1
     pl.when(seq >= turn)(relay)
 
+    def multiply(t, dest, slot, part):
+        @pl.loop(0, width // tile)
+        def _(i):
+            cols = pl.ds(pl.multiple_of(i * tile, tile), tile)
+            dest[slot, part, cols] = jnp.dot(
+                gained_ref[part, :], wbuf[t, :, cols], preferred_element_type=jnp.float32
+            ).astype(jnp.bfloat16)
+
+    def y_copy(s, c):
+        part = pl.ds(c * rows, rows)
+        return pltpu.make_async_remote_copy(
+            src_ref=peer_out.at[s, part],
+            dst_ref=peer_in.at[s, part],
+            send_sem=y_send.at[s, c],
+            recv_sem=y_recv.at[s, c],
+            device_id={"mp": zm * PAIRS + 1 - ym},
+            device_id_type=MESH,
+        )
+
+    sent = 0
     state = relay_in[...].astype(jnp.float32)
     for b in range(blocks):
         span = slice(b * BLOCK, (b + 1) * BLOCK)
@@ -228,31 +261,16 @@
             squared = squared + gated * gated
             gained_ref[span, cols] = (gated * gain_ref[:, cols]).astype(jnp.bfloat16)
         square_sum[span, :] = squared
+        if b == 0:
+            w_copy(0).wait()
+        multiply(0, peer_out, 0, span)
+        while sent < CHUNKS and (sent + 1) * rows <= (b + 1) * BLOCK:
+            y_copy(0, sent).start()
+            sent += 1
         if b < blocks - 1:
             state = block_decay(b) * state + local[b]
     total_row = jnp.sum(jnp.transpose(square_sum[...]), axis=0, keepdims=True)
     squares_ref[...] = jnp.broadcast_to(total_row, (8, tokens))
-
-    def multiply(t, dest, slot):
-        w_copy(t).wait()
-
-        @pl.loop(0, width // tile)
-        def _(i):
-            cols = pl.ds(pl.multiple_of(i * tile, tile), tile)
-            dest[slot, :, cols] = jnp.dot(
-                gained_ref[...], wbuf[t, :, cols], preferred_element_type=jnp.float32
-            ).astype(jnp.bfloat16)
-
-    def y_copy(s, c):
-        part = pl.ds(c * rows, rows)
-        return pltpu.make_async_remote_copy(
-            src_ref=peer_out.at[s, part],
-            dst_ref=peer_in.at[s, part],
-            send_sem=y_send.at[s, c],
-            recv_sem=y_recv.at[s, c],
-            device_id={"mp": zm * PAIRS + 1 - ym},
-            device_id_type=MESH,
-        )
 
     def sq_copy(d):
         return pltpu.make_async_remote_copy(
@@ -287,15 +305,86 @@
             device_id_type=MESH,
         )
 
+    for d in range(1, count):
+        sq_copy(d).start()
+
+    def line_copy(s, e, way):
+        dest = ((from_low, line_low), (from_high, line_high))[way < 0][e]
+        sems = line_low_recv if way > 0 else line_high_recv
+        z = targets[s]
+        return pltpu.make_async_remote_copy(
+            src_ref=(own, peer_out)[e].at[s, line_part],
+            dst_ref=dest.at[z, line_part] if e == 0 else dest.at[z],
+            send_sem=line_send.at[s, e],
+            recv_sem=sems.at[z, e],
+            device_id={"mp": (zm + way) * PAIRS + ym},
+            device_id_type=MESH,
+        )
+
+    def line_arrival(s, e, way):
+        dest = ((from_low, line_low), (from_high, line_high))[way < 0][e]
+        sems = line_low_recv if way > 0 else line_high_recv
+        z = targets[s]
+        return pltpu.make_async_remote_copy(
+            src_ref=(own, peer_out)[e].at[s, line_part],
+            dst_ref=dest.at[z, line_part] if e == 0 else dest.at[z],
+            send_sem=line_send.at[s, e],
+            recv_sem=sems.at[z, e],
+            device_id={"mp": (zm - way) * PAIRS + ym},
+            device_id_type=MESH,
+        )
+
+    def cross_copy():
+        return pltpu.make_async_remote_copy(
+            src_ref=peer_out.at[lines - 1, line_part],
+            dst_ref=peer_in.at[lines - 1, line_part],
+            send_sem=cross_send.at[0],
+            recv_sem=cross_recv.at[0],
+            device_id={"mp": zm * PAIRS + 1 - ym},
+            device_id_type=MESH,
+        )
+
+    def line_step(s):
+        z = targets[s]
+        for e in (1, 0):
+            mine = (own, peer_out)[e]
+            line_total[...] = mine[s, line_part, :].astype(jnp.float32)
+
+            @pl.when(jnp.logical_and(z >= zm, zm > 0))
+            def _():
+                line_arrival(s, e, 1).wait_recv()
+                came = from_low[z, line_part, :] if e == 0 else line_low[z]
+                line_total[...] += came.astype(jnp.float32)
+
+            @pl.when(jnp.logical_and(z <= zm, zm < lines - 1))
+            def _():
+                line_arrival(s, e, -1).wait_recv()
+                came = from_high[z, line_part, :] if e == 0 else line_high[z]
+                line_total[...] += came.astype(jnp.float32)
+
+            if s < lines - 1:
+                mine[s, line_part, :] = line_total[...].astype(jnp.bfloat16)
+
+                @pl.when(z > zm)
+                def _():
+                    line_copy(s, e, 1).start()
+
+                @pl.when(z < zm)
+                def _():
+                    line_copy(s, e, -1).start()
+            elif e == 1:
+                mine[s, line_part, :] = line_total[...].astype(jnp.bfloat16)
+                cross_copy().start()
+
+    everything = slice(0, tokens)
     for s in range(lines):
-        multiply(s, peer_out, s)
-        for c in range(CHUNKS):
-            y_copy(s, c).start()
-        if s == 0:
-            for d in range(1, count):
-                sq_copy(d).start()
-    for s in range(lines):
-        multiply(lines + s, own, s)
+        if s > 0:
+            w_copy(s).wait()
+            multiply(s, peer_out, s, everything)
+            for c in range(CHUNKS):
+                y_copy(s, c).start()
+        w_copy(lines + s).wait()
+        multiply(lines + s, own, s, everything)
 
     squares = squares_ref[...]
     for d in range(1, count):
@@ -307,6 +396,8 @@
 
     for s in range(lines):
         z = targets[s]
+        for early in range(2 * s, min(2 * s + 2, lines)):
+            line_step(early)
         for c in range(CHUNKS):
             part = pl.ds(c * rows, rows)
             y_copy(s, c).wait_recv()
@@ -339,6 +430,26 @@
                 for k in range(width // 128):
                     cols = slice(k * 128, (k + 1) * 128)
                     out_ref[part, cols] = (total[:, cols] * factor).astype(jnp.bfloat16)
+
+    cross_copy().wait_recv()
+    line_total[...] += peer_in[lines - 1, line_part, :].astype(jnp.float32)
+    factor = scaling[tokens - line_rows :]
+    for k in range(width // 128):
+        cols = slice(k * 128, (k + 1) * 128)
+        out_ref[line_part, cols] = (line_total[:, cols] * factor).astype(jnp.bfloat16)
+
+    cross_copy().wait_send()
+    for s in range(lines - 1):
+        z = targets[s]
+        for e in (0, 1):
+
+            @pl.when(z > zm)
+            def _():
+                line_copy(s, e, 1).wait_send()
+
+            @pl.when(z < zm)
+            def _():
+                line_copy(s, e, -1).wait_send()
 
     @pl.when(seq < seq_count - 1)
     def _():
@@ -386,19 +497,20 @@
     out_weight,
 ):
     tokens, depth = signal.shape
-    heads = log_decay.shape[1]
     state_width = input_map.shape[1]
     count = lax.axis_size("mp")
     lines = count // PAIRS
+    line_rows = tokens // LINE_SHARE
     width = out_weight.shape[1] // count
-    skip_lanes = jnp.repeat(skip_gain, depth // heads)[None]
     dma = pltpu.SemaphoreType.DMA
     held = lambda n: pltpu.VMEM((n, tokens, width), jnp.bfloat16)
     whole = pl.BlockSpec(memory_space=pltpu.VMEM)
     return pl.pallas_call(
         layer_kernel,
         out_shape=jax.ShapeDtypeStruct((tokens, width), jnp.bfloat16),
-        in_specs=[whole] * 8 + [pl.BlockSpec(memory_space=pl.ANY)],
+        in_specs=[whole] * 6
+        + [pl.BlockSpec(memory_space=pltpu.SMEM), whole]
+        + [pl.BlockSpec(memory_space=pl.ANY)],
         out_specs=whole,
         scratch_shapes=[
             pltpu.VMEM((tokens, depth), jnp.bfloat16),
@@ -409,13 +521,16 @@
             pltpu.VMEM((state_width, depth), jnp.bfloat16),
             pltpu.VMEM((state_width, depth), jnp.bfloat16),
             pltpu.VMEM((tokens, LANES), jnp.float32),
+            pltpu.VMEM((line_rows, width), jnp.float32),
+            pltpu.VMEM((lines, line_rows, width), jnp.bfloat16),
+            pltpu.VMEM((lines, line_rows, width), jnp.bfloat16),
             pltpu.VMEM((2 * lines, depth, width), jnp.bfloat16),
             held(lines),
             held(lines),
             held(lines),
             held(lines),
             held(lines),
-            pltpu.VMEM((tokens // CHUNKS, width), jnp.float32),
+            pltpu.VMEM(((tokens - line_rows) // CHUNKS, width), jnp.float32),
             pltpu.VMEM((count, 8, tokens), jnp.float32),
             dma((2 * lines,)),
             dma((lines, CHUNKS)),
@@ -427,6 +542,11 @@
             dma((count,)),
             dma((RELAY_CHUNKS,)),
             dma((RELAY_CHUNKS,)),
+            dma((lines, 2)),
+            dma((lines, 2)),
+            dma((lines, 2)),
+            dma((1,)),
+            dma((1,)),
         ],
         compiler_params=pltpu.CompilerParams(
             collective_id=0, has_side_effects=True, vmem_limit_bytes=58 << 20
@@ -439,7 +559,7 @@
         output_map,
         jnp.transpose(log_decay),
         jnp.transpose(step_size),
-        skip_lanes,
+        skip_gain,
         norm_gain[None],
         out_weight,
     )

time: 120 us -> 123 us (1.025)
  Pallas kernels: 114 us -> 119 us
  local copies, waits for them, and re-layouts: 3.66 us -> 2.26 us
    pallas_call x1, Pallas kernels: 114 us -> 119 us  [on_device(): pl.pallas_call(layer_kernel, out_shape=jax.ShapeDtypeStruct((tokens, widt...]
where the time goes in v3:
time: 123 us; the launch traced here: 122 us
  Pallas kernels  119 us (97%)
  local copies, waits for them, and re-layouts  2.26 us (2%)
    pallas_call x1, Pallas kernels, on_device(): pl.pallas_call(layer_kernel, out_shape=jax.ShapeDtypeStruct((tokens, widt...  119 us

profile of v3, /device:TPU:22, one launch (start us, length us, event | category | flops | bytes accessed | tf_op | source)
XLA Modules:
  0.0 121.7 jit_solution(2864793670198032232)
XLA Ops:
  0.0 119.4 %layer.1 = bf16[512,1024]{1,0:T(8,128)(2,1)} custom-call(bf16[512,1024]{1,0:T(8,128)(2,1)} %signal_ref.1, bf16[512,1024]{1,0:T(8,128)(2,1)} %gate_ref.1, bf16[512,128]{1,0:T(8,128)(2,1)} %keys_ref.1, bf16[512,128]{1,0:T(8,128)(2,1)} %query_ref.1, f32[16,512]{1,0:T(8,128)} %bitcast.3, f32[16,512]{1,0:T(8,128)} %bitcast.4, f32[16]{0:T(128)} %skip_ref.1, ...), custom_call_target="tpu_custom_call" | custom-call | tf_op jit(solution)/shard_map/layer/pallas_call | solution.py:508
  119.4 2.3 %copy.11 = bf16[512,1024]{1,0:T(8,128)(2,1)} copy(bf16[512,1024]{1,0:T(8,128)(2,1)} %layer.1) | data formatting | bytes 2097152

commit v4 on v3

--- a/solution.py
+++ b/solution.py
@@ -103,8 +103,9 @@
         cols = pl.ds(pl.multiple_of(columns[t] * width, width), width)
         return pltpu.make_async_copy(weight_ref.at[:, cols], wbuf.at[t], w_sem.at[t])
 
-    for t in range(2 * lines):
+    for t in range(lines):
         w_copy(t).start()
+        w_copy(lines + t).start()
 
     heads = decay_ref.shape[0]
     width_in = signal_ref.shape[1]
@@ -376,8 +377,8 @@
                 mine[s, line_part, :] = line_total[...].astype(jnp.bfloat16)
                 cross_copy().start()
 
-    everything = slice(0, tokens)
-    for s in range(lines):
+    def feed_step(s):
+        everything = slice(0, tokens)
         if s > 0:
             w_copy(s).wait()
             multiply(s, peer_out, s, everything)
@@ -385,6 +386,10 @@
                 y_copy(s, c).start()
         w_copy(lines + s).wait()
         multiply(lines + s, own, s, everything)
+        line_step(s)
+
+    feed_step(0)
+    feed_step(1)
 
     squares = squares_ref[...]
     for d in range(1, count):
@@ -396,8 +401,8 @@
 
     for s in range(lines):
         z = targets[s]
-        for early in range(2 * s, min(2 * s + 2, lines)):
-            line_step(early)
+        if 0 < s < lines - 1:
+            feed_step(s + 1)
         for c in range(CHUNKS):
             part = pl.ds(c * rows, rows)
             y_copy(s, c).wait_recv()

time: 123 us -> 116 us (0.943); the launches traced: 122 us -> 116 us
  Pallas kernels: 119 us -> 114 us
    pallas_call x1, Pallas kernels: 119 us -> 114 us  [on_device(): pl.pallas_call(layer_kernel, out_shape=jax.ShapeDtypeStruct((tokens, widt...]
where the time goes in v4:
time: 116 us
  Pallas kernels  114 us (98%)
  local copies, waits for them, and re-layouts  2.26 us (2%)
    pallas_call x1, Pallas kernels, on_device(): pl.pallas_call(layer_kernel, out_shape=jax.ShapeDtypeStruct((tokens, widt...  114 us

profile of v4, /device:TPU:22, one launch (start us, length us, event | category | flops | bytes accessed | tf_op | source)
XLA Modules:
  0.0 116.1 jit_solution(16874462918425205289)
XLA Ops:
  0.0 113.8 %layer.1 = bf16[512,1024]{1,0:T(8,128)(2,1)} custom-call(bf16[512,1024]{1,0:T(8,128)(2,1)} %signal_ref.1, bf16[512,1024]{1,0:T(8,128)(2,1)} %gate_ref.1, bf16[512,128]{1,0:T(8,128)(2,1)} %keys_ref.1, bf16[512,128]{1,0:T(8,128)(2,1)} %query_ref.1, f32[16,512]{1,0:T(8,128)} %bitcast.3, f32[16,512]{1,0:T(8,128)} %bitcast.4, f32[16]{0:T(128)} %skip_ref.1, ...), custom_call_target="tpu_custom_call" | custom-call | tf_op jit(solution)/shard_map/layer/pallas_call | solution.py:513
  113.9 2.3 %copy.11 = bf16[512,1024]{1,0:T(8,128)(2,1)} copy(bf16[512,1024]{1,0:T(8,128)(2,1)} %layer.1) | data formatting | bytes 2097152

commit v5 on v4

--- a/solution.py
+++ b/solution.py
@@ -7,7 +7,7 @@
 
 BLOCK = 256
 PAIRS = 2
-CHUNKS = 4
+CHUNKS = 7
 RELAY_CHUNKS = 2
 LINE_SHARE = 8
 LANES = 128

time: 116 us -> 117 us (level)
  no operation moved by 1% of the time
where the time goes in v5:
time: 117 us
  Pallas kernels  114 us (97%)
  local copies, waits for them, and re-layouts  2.26 us (2%)
    pallas_call x1, Pallas kernels, on_device(): pl.pallas_call(layer_kernel, out_shape=jax.ShapeDtypeStruct((tokens, widt...  114 us

profile of v5, /device:TPU:22, one launch (start us, length us, event | category | flops | bytes accessed | tf_op | source)
XLA Modules:
  0.0 116.6 jit_solution(15382198937432794053)
XLA Ops:
  0.0 114.4 %layer.1 = bf16[512,1024]{1,0:T(8,128)(2,1)} custom-call(bf16[512,1024]{1,0:T(8,128)(2,1)} %signal_ref.1, bf16[512,1024]{1,0:T(8,128)(2,1)} %gate_ref.1, bf16[512,128]{1,0:T(8,128)(2,1)} %keys_ref.1, bf16[512,128]{1,0:T(8,128)(2,1)} %query_ref.1, f32[16,512]{1,0:T(8,128)} %bitcast.3, f32[16,512]{1,0:T(8,128)} %bitcast.4, f32[16]{0:T(128)} %skip_ref.1, ...), custom_call_target="tpu_custom_call" | custom-call | tf_op jit(solution)/shard_map/layer/pallas_call | solution.py:513
  114.4 2.3 %copy.11 = bf16[512,1024]{1,0:T(8,128)(2,1)} copy(bf16[512,1024]{1,0:T(8,128)(2,1)} %layer.1) | data formatting | bytes 2097152
